TPU v7x, 512 devices: a whole 4x4x16 slice. The times are simulated.
512 devices in a mesh: grp: 16 (over z), mem: 32 (over y, x, core).
Axes of the slice: x: 4, y: 4, z: 16, core: 2. Of those that a mesh axis runs over, the one named last changes fastest.
Arguments:
- bin_sketch: bfloat16 [4096, 1024], P(('grp', 'mem')), may hold values from -6 to 6
- rep_sketch: bfloat16 [131072, 1024], P(('grp', 'mem')), may hold values from -6 to 6
- bin_profile: bfloat16 [4096, 32768], P('grp', 'mem'), may hold values from -6 to 6
- member_profile: bfloat16 [48, 256, 32768], P('grp', None, 'mem'), may hold values from -6 to 6
- bin_routes: int32 [4096, 2], P('grp'), may hold values from 0 to 47, all different within a row; in each aligned block of 256 rows (0 to 255, 256 to 511, ...) at most 16 rows name the same one
- owner_slot: int32 [48], replicated, may hold values from 0 to 47, each once
- cluster_sizes: int32 [48], replicated, may hold values from 128 to 256, as said below
Outputs:
- coarse_scores: bfloat16 [4096, 131072], P(None, ('grp', 'mem'))
- fine_scores: float32 [4096, 2, 256], P('grp', None, 'mem')
Inputs may be any that keep to these rules, and one draw needn't show every extreme that they name: `bin_routes`: within the bins of one index of grp (256 consecutive bins), no cluster is named by more than 16 routes, a bound that some block reaches; the two clusters of a bin differ. `owner_slot`: A permutation. `cluster_sizes`: each a multiple of 128.
All inputs are finite; a program needn't handle non-finite values.
Results may differ from a plain program's by a relative error of at most 0.001.
Values may be sent and summed in bfloat16 or wider, within the bound.
A program may use at most 128 MiB of HBM per device.

v0:
```python
import jax
import jax.numpy as jnp
from jax import lax
from jax.sharding import PartitionSpec as P

FW = 32768
MOST = 16


def from_everyone(array, axis):
    length = lax.axis_size(axis)
    return lax.all_to_all(
        jnp.broadcast_to(array[None], (length, *array.shape)), axis, 0, 0, tiled=True
    )


def joined_along(parts, dim):
    parts = jnp.moveaxis(parts, 0, dim)
    lengths = parts.shape
    return parts.reshape(*lengths[:dim], lengths[dim] * lengths[dim + 1], *lengths[dim + 2 :])


def collect(array, axis, dim):
    parts = from_everyone(array, axis)
    return joined_along(parts, dim)


def cut_along(array, dim, length):
    lengths = array.shape
    parts = array.reshape(*lengths[:dim], length, lengths[dim] // length, *lengths[dim + 1 :])
    return jnp.moveaxis(parts, dim, 0)


def summed_on_arrival(array, axis, dim):
    length = lax.axis_size(axis)
    parts = lax.all_to_all(cut_along(array, dim, length), axis, 0, 0, tiled=True)
    return jnp.sum(parts, axis=0)


def local(
    bin_sketch, rep_sketch, bin_profile, member_profile, bin_routes, owner_slot, cluster_sizes
):
    coarse_scale = bin_sketch.shape[1] ** (-0.5)
    group_rows = collect(bin_sketch, "mem", 0)
    product = lax.dot_general(
        lax.all_gather(group_rows, "grp", axis=0, tiled=True),
        rep_sketch,
        (((1,), (1,)), ((), ())),
        preferred_element_type=jnp.float32,
    )
    coarse_scores = (product * coarse_scale).astype(jnp.bfloat16)
    rows_here, width_here = bin_profile.shape
    slot_count, members, _ = member_profile.shape
    groups = lax.axis_size("grp")
    cluster_total = owner_slot.shape[0]
    capacity = groups * slot_count * MOST
    route_flat = bin_routes.reshape(-1)
    cluster_ids = jnp.arange(cluster_total, dtype=jnp.int32)
    route_hit = (route_flat[:, None] == cluster_ids[None, :]).astype(jnp.int32)
    storage = jnp.sum(route_hit * owner_slot[None, :], axis=1)
    route_size = jnp.sum(route_hit * cluster_sizes[None, :], axis=1)
    route_rank = jnp.sum((jnp.cumsum(route_hit, axis=0) - route_hit) * route_hit, axis=1)
    slot_index = storage * MOST + route_rank
    source = bin_profile[jnp.arange(route_flat.shape[0], dtype=jnp.int32) // 2]
    outgoing = jnp.zeros((capacity, width_here), jnp.bfloat16).at[slot_index].set(source)
    outgoing = outgoing.reshape(groups, slot_count * MOST, width_here)
    incoming = lax.all_to_all(outgoing, "grp", split_axis=0, concat_axis=0, tiled=True)
    incoming = incoming.reshape(groups, slot_count, MOST, width_here)
    partial_value = jnp.einsum(
        "gsmc,sjc->gsmj", incoming, member_profile, preferred_element_type=jnp.float32
    )
    summed = summed_on_arrival(partial_value, "mem", 3)
    returned = lax.all_to_all(summed, "grp", split_axis=0, concat_axis=0, tiled=True)
    member_local = returned.shape[3]
    route_scores = returned.reshape(capacity, member_local)[slot_index] * FW ** (-0.5)
    column = lax.axis_index("mem") * member_local + jnp.arange(member_local, dtype=jnp.int32)
    member_live = column[None, :] < route_size[:, None]
    fine_scores = jnp.where(member_live, route_scores, 0.0).reshape(rows_here, 2, member_local)
    return (coarse_scores, fine_scores)


def solution(mesh):
    return jax.shard_map(
        local,
        mesh=mesh,
        in_specs=(
            P(("grp", "mem"), None),
            P(("grp", "mem"), None),
            P("grp", "mem"),
            P("grp", None, "mem"),
            P("grp", None),
            P(),
            P(),
        ),
        out_specs=(P(None, ("grp", "mem")), P("grp", None, "mem")),
        check_vma=False,
    )
```

profile of v0, /device:TPU:1, one launch (start us, length us, event | category | flops | bytes accessed | tf_op | source)
XLA Modules:
  0.0 224.5 jit_solution(15399762834243814376)
XLA Ops:
  7.3 0.9 broadcast_in_dim.7
  8.1 21.7 %all_to_all.20 = bf16[32,8,1024]{2,1,0:T(8,128)(2,1)} all-to-all(bf16[32,8,1024]{2,1,0:T(8,128)(2,1)S(1)} %broadcast_in_dim.7), channel_id=1, replica_groups=mesh['grp'=16,'mem'=32] {'mem'}, dimensions={0} | all-to-all | bytes 1048576 | tf_op jit(solution)/shard_map/all_to_all | solution.py:12
  30.3 1.2 reduce-window.6
  31.5 0.2 slice_reduce_fusion
  32.0 7.4 %scatter_custom_fusion = bf16[768,1024]{1,0:T(8,128)(2,1)S(1)} fusion(s32[512]{0:T(512)S(1)} %bitcast.56, bf16[256,1024]{1,0:T(8,128)(2,1)} %param.9, s32[1024]{0:T(1024)S(1)} %pad_clamp_fusion.1, bf16[]{:T(256)} %constant.36.clone.1), kind=kCustom, calls=%fused_computation.9 | custom fusion | bytes 1573376 | tf_op jit(solution)/shard_map/scatter | solution.py:65
  39.4 100.3 %all_to_all.21 = bf16[16,48,1024]{2,1,0:T(8,128)(2,1)S(1)} all-to-all(bf16[16,48,1024]{2,1,0:T(8,128)(2,1)S(1)} %bitcast.50), channel_id=1, replica_groups=mesh['grp'=16,'mem'=32] {'grp'}, dimensions={0} | all-to-all | bytes 3145728 | tf_op jit(solution)/shard_map/all_to_all | solution.py:67
  139.7 0.6 fusion.4
  140.4 4.0 %copy.22 = f32[16,3,16,256]{2,3,1,0:T(8,128)} copy(f32[16,3,16,256]{3,2,0,1:T(8,128)S(1)} %fusion.4) | data formatting | bytes 1572864 | tf_op jit(solution)/shard_map/gsmc,sjc->gsmj/transpose | solution.py:69
  144.4 6.2 %copy_bitcast_fusion = f32[32,16,3,8,16]{4,3,2,1,0:T(8,128)} fusion(f32[16,3,16,256]{2,3,1,0:T(8,128)} %copy.22), kind=kLoop, calls=%fused_computation.36 | loop fusion | bytes 1572864
  150.5 5.5 %reshape.165 = f32[32,1,6144]{2,1,0:T(1,128)} reshape(f32[32,16,3,8,16]{4,3,2,1,0:T(8,128)} %copy_bitcast_fusion) | data formatting | bytes 1572864
  156.0 5.4 %all-to-all-start.2 = ((f32[32,1,6144]{2,1,0:T(1,128)}), f32[32,1,6144]{2,1,0:T(1,128)S(1)}, u32[]{:S(2)}, u32[]{:S(2)}) async-start(f32[32,1,6144]{2,1,0:T(1,128)} %reshape.165), calls=%async_computation.2 | async-start | bytes 1572864 | tf_op jit(solution)/shard_map/all_to_all | solution.py:36
  161.6 14.1 %all-to-all-done.2 = f32[32,1,6144]{2,1,0:T(1,128)S(1)} async-done(((f32[32,1,6144]{2,1,0:T(1,128)}), f32[32,1,6144]{2,1,0:T(1,128)S(1)}, u32[]{:S(2)}, u32[]{:S(2)}) %all-to-all-start.2) | async-done | bytes 786464 | tf_op jit(solution)/shard_map/all_to_all | solution.py:36
  175.7 0.5 broadcast.141
  176.2 2.6 %reduce.2 = f32[32,6144]{1,0:T(8,128)S(1)} reduce(f32[32,1,6144]{2,1,0:T(1,128)S(1)} %all-to-all-done.2, f32[]{:T(128)} %broadcast.141), dimensions={1}, to_apply=%all_to_all.14.reduce_sub_computation | reduce | bytes 1572868 | tf_op jit(solution)/shard_map/all_to_all | solution.py:36
  178.8 3.9 %reshape.166 = f32[32,16,3,8,16]{4,3,2,1,0:T(8,128)} reshape(f32[32,6144]{1,0:T(8,128)S(1)} %reduce.2) | data formatting | bytes 1572864
  182.7 3.3 %bitcast_reduce_fusion = f32[16,3,16,8]{2,3,1,0:T(8,128)S(1)} fusion(f32[32,16,3,8,16]{4,3,2,1,0:T(8,128)} %reshape.166), kind=kLoop, calls=%fused_computation.35 | loop fusion | flops 190464 | bytes 811008 | tf_op jit(solution)/shard_map/reduce_sum | solution.py:37
  186.0 0.7 reshape.167
  186.8 9.3 %all-to-all-start.3 = ((f32[16,1,384]{2,1,0:T(1,128)}), f32[16,1,384]{2,1,0:T(1,128)S(1)}, u32[]{:S(2)}, u32[]{:S(2)}) async-start(f32[16,1,384]{2,1,0:T(1,128)} %reshape.167), calls=%async_computation.3 | async-start | bytes 49152 | tf_op jit(solution)/shard_map/all_to_all | solution.py:73
  196.1 11.5 %all-to-all-done.3 = f32[16,1,384]{2,1,0:T(1,128)S(1)} async-done(((f32[16,1,384]{2,1,0:T(1,128)}), f32[16,1,384]{2,1,0:T(1,128)S(1)}, u32[]{:S(2)}, u32[]{:S(2)}) %all-to-all-start.3) | async-done | bytes 24608 | tf_op jit(solution)/shard_map/all_to_all | solution.py:73
  207.7 0.7 reduce.3
  208.5 0.2 copy.25
  208.7 1.0 gather_fusion
  209.9 0.7 compare_select_fusion
  210.6 7.1 %fusion = bf16[4096,256]{1,0:T(8,128)(2,1)} fusion(bf16[4096,1024]{1,0:T(8,128)(2,1)} %all-gather.2.cloned.1.call-done, bf16[256,1024]{1,0:T(8,128)(2,1)S(1)} %copy-done.4), kind=kOutput, calls=%fused_computation.4 | convolution fusion | flops 2149580800 | bytes 11010048 | tf_op jit(solution)/shard_map/dot_general | solution.py:45
  (31 shorter events, 1.2 us)
Async XLA Ops:
  7.2 132.6 %copy-start = (bf16[3,256,1024]{2,1,0:T(8,128)(2,1)S(1)}, bf16[3,256,1024]{2,1,0:T(8,128)(2,1)}, u32[]{:S(2)}) copy-start(bf16[3,256,1024]{2,1,0:T(8,128)(2,1)} %param.10) | copy-start | bytes 4718596
  7.2 22.7 %copy-start.1 = (s32[256,2]{0,1:T(2,128)S(1)}, s32[256,2]{0,1:T(2,128)}, u32[]{:S(2)}) copy-start(s32[256,2]{0,1:T(2,128)} %param.11) | copy-start | bytes 6148
  7.2 24.6 %copy-start.3 = (s32[48]{0:T(128)S(1)}, s32[48]{0:T(128)}, u32[]{:S(2)}) copy-start(s32[48]{0:T(128)} %param.12) | copy-start | bytes 580
  7.2 24.6 %copy-start.2 = (s32[48]{0:T(128)S(1)}, s32[48]{0:T(128)}, u32[]{:S(2)}) copy-start(s32[48]{0:T(128)} %param.13) | copy-start | bytes 580
  7.2 203.4 %all-gather.2.cloned.1.call-start = ((), (), s32[]{:S(2)}) async-start(), calls=%async_computation.4 | async-start | bytes 8912896 | tf_op jit(solution)/shard_map/all_gather | solution.py:46
  156.0 19.7 %all-to-all-start.2 = ((f32[32,1,6144]{2,1,0:T(1,128)}), f32[32,1,6144]{2,1,0:T(1,128)S(1)}, u32[]{:S(2)}, u32[]{:S(2)}) async-start(f32[32,1,6144]{2,1,0:T(1,128)} %reshape.165), calls=%async_computation.2 | async-start | bytes 1572864 | tf_op jit(solution)/shard_map/all_to_all | solution.py:36
  186.8 23.8 %copy-start.4 = (bf16[256,1024]{1,0:T(8,128)(2,1)S(1)}, bf16[256,1024]{1,0:T(8,128)(2,1)}, u32[]{:S(2)}) copy-start(bf16[256,1024]{1,0:T(8,128)(2,1)} %param.8) | copy-start | bytes 1572868
  186.8 20.9 %all-to-all-start.3 = ((f32[16,1,384]{2,1,0:T(1,128)}), f32[16,1,384]{2,1,0:T(1,128)S(1)}, u32[]{:S(2)}, u32[]{:S(2)}) async-start(f32[16,1,384]{2,1,0:T(1,128)} %reshape.167), calls=%async_computation.3 | async-start | bytes 49152 | tf_op jit(solution)/shard_map/all_to_all | solution.py:73
Sparse Core Ops, SparseCore 0:
  30.0 172.0 all-gather.1
where the time goes:
time: 225 us
  blocking collectives  122 us (54%)
  local copies, waits for them, and re-layouts  31.4 us (14%)
  waiting for transfers between devices  25.7 us (11%)
  starting transfers between devices  14.7 us (7%)
  between operations  14.3 us (6%)
  other arithmetic  8.71 us (4%)
  matrix products  7.71 us (3%)
    all_to_all x1, blocking collectives, local(): lax.all_to_all(outgoing, 'grp', split_axis=0, concat_axis=0, tiled=True)  100 us
    all_to_all x1, blocking collectives, from_everyone(): lax.all_to_all(jnp.broadcast_to(array[None], (length, *array.shape)), axi...  21.7 us
    unnamed x16, local copies, waits for them, and re-layouts  16.6 us
    all_to_all x1, waiting for transfers between devices, summed_on_arrival(): lax.all_to_all(cut_along(array, dim, length), axis, 0, 0, tiled=True)  14.1 us
    all_to_all x1, waiting for transfers between devices, local(): lax.all_to_all(summed, 'grp', split_axis=0, concat_axis=0, tiled=True)  11.5 us
    all_to_all x1, starting transfers between devices, local(): lax.all_to_all(summed, 'grp', split_axis=0, concat_axis=0, tiled=True)  9.34 us
    scatter x1, local copies, waits for them, and re-layouts, local(): jnp.zeros((capacity, width_here), jnp.bfloat16).at[slot_index].set(source)  7.43 us
    dot_general x1, matrix products, local(): lax.dot_general(lax.all_gather(group_rows, 'grp', axis=0, tiled=True), re...  7.1 us
  transfers between devices with their start and end apart: 3, of which 2 were waited for; matrix products, arithmetic and copies ran while one was open for 18% of the time, Pallas kernels for 0%

commit v1 on v0

v1 whole, which is shorter than its diff:
```python
import functools

import jax
import jax.numpy as jnp
from jax import lax
from jax.experimental import pallas as pl
from jax.experimental.pallas import tpu as pltpu
from jax.sharding import PartitionSpec as P

MOST = 16
RAW = 3
CHUNKS = 8
QUEUE = 3
BF = jnp.bfloat16
F32 = jnp.float32
I32 = jnp.int32


def compact_list(half, raw):
    return [(h, d) for h in range(raw + 1, half + 1) for d in range(half, h - 1, -1)]


def screen(cfg, bs_ref, rep_hbm, bp_ref, mp_hbm, v_ref, out_ref, fine_ref, *scratch):
    n, m_all, edge, raw_hops = cfg["n"], cfg["m"], cfg["edge"], cfg["raw"]
    (ring, vbuf, cbuf, dbuf, ext, gat, rep, mp, stage, part, red, sums, ret,
     zs, zr, xs, xr, rs, rr, ts, tr, ls, os_) = scratch
    half = n // 2
    messages = compact_list(half, raw_hops)
    grp = lax.axis_index("grp")
    mem = lax.axis_index("mem")
    core = lax.rem(mem, 2)
    sigma = 1 - 2 * core
    chip = mem // 2
    y, x = chip // edge, lax.rem(chip, edge)
    alpha = jnp.where(core == 0, x, y)
    beta = jnp.where(core == 0, y, x)
    bins = bp_ref.shape[0]
    width = bp_ref.shape[1]
    rows = bins // CHUNKS
    slots = mp.shape[0]
    block = slots * MOST

    def group_at(sign, distance):
        return lax.rem(grp + sigma * (sign * distance) + n, n)

    def z_device(sign):
        return {"grp": group_at(sign, 1), "mem": mem}

    def member_at(a, b):
        yy = jnp.where(core == 0, b, a)
        xx = jnp.where(core == 0, a, b)
        return (yy * edge + xx) * 2 + core

    def a_device(i):
        return {"grp": grp, "mem": member_at(lax.rem(alpha + i, edge), beta)}

    def b_device(i):
        return {"grp": grp, "mem": member_at(alpha, lax.rem(beta + i, edge))}

    partner = {"grp": grp, "mem": mem + sigma}

    greeted = [z_device(1), z_device(-1), partner]
    greeted += [a_device(i) for i in range(1, edge)] + [b_device(i) for i in range(1, edge)]
    barrier = pltpu.get_barrier_semaphore()
    for device in greeted:
        pl.semaphore_signal(barrier, inc=1, device_id=device, device_id_type=pl.DeviceIdType.MESH)
    rep_copy = pltpu.make_async_copy(rep_hbm, rep, ls.at[0])
    mp_copy = pltpu.make_async_copy(mp_hbm, mp, ls.at[1])
    rep_copy.start()
    mp_copy.start()
    own_copy = pltpu.make_async_copy(bs_ref, gat.at[grp, core, beta, alpha], ls.at[2])
    own_copy.start()
    pl.semaphore_wait(barrier, len(greeted))

    def remote(src, dst, send_sem, recv_sem, device):
        return pltpu.make_async_remote_copy(
            src_ref=src, dst_ref=dst, send_sem=send_sem, recv_sem=recv_sem,
            device_id=device, device_id_type=pl.DeviceIdType.MESH)

    class Ring:
        def __init__(self, index, sign):
            self.index, self.sign = index, sign
            self.sent, self.done = [], 0
            self.coarse, self.idx, self.raw, self.compact = {}, {}, {}, {}

        def send(self, src, dst):
            k = len(self.sent)
            if k - self.done >= QUEUE:
                self.sent[self.done].wait_send()
                self.done += 1
            copy = remote(src, dst, zs.at[self.index, k], zr.at[self.index, k], z_device(self.sign))
            copy.start()
            self.sent.append(copy)
            return copy

        def drain(self):
            while self.done < len(self.sent):
                self.sent[self.done].wait_send()
                self.done += 1

        def coarse_hops(self):
            return half if self.index == 0 else half - 1

        def send_coarse(self, h):
            if h > self.coarse_hops():
                return
            source = group_at(-self.sign, h - 1)
            place = gat.at[source, core, beta, alpha]
            self.coarse[h] = self.send(bs_ref if h == 1 else place, place)

        def send_idx(self, h):
            src = v_ref if h == 1 else vbuf.at[self.index, h - 2]
            self.idx[h] = self.send(src, vbuf.at[self.index, h - 1])

        def send_raw(self, r):
            if r < CHUNKS:
                src = bp_ref.at[pl.ds(r * rows, rows), :]
            else:
                src = ring.at[self.index, r - CHUNKS]
            self.raw[r] = self.send(src, ring.at[self.index, r])

        def tail_rows(self, d):
            if d < half:
                return 0, block
            first = (slots - slots // 3) * MOST
            return (0, first) if self.index == 0 else (first, block - first)

        def send_compact(self, k):
            h, d = messages[k]
            _, count = self.tail_rows(d)
            if h == raw_hops + 1:
                src = dbuf.at[self.index, half - d, pl.ds(0, count)]
            else:
                before = messages.index((h - 1, d))
                self.compact[before].wait_recv()
                src = cbuf.at[self.index, before, pl.ds(0, count)]
            self.compact[k] = self.send(src, cbuf.at[self.index, k, pl.ds(0, count)])

    rings = [Ring(0, 1), Ring(1, -1)]

    def source_of(ring_, h):
        return group_at(-ring_.sign, h)

    def spread_copies(source, slot, phase):
        copies = []
        if phase == 0:
            place = gat.at[source, core, beta, alpha]
            for i in range(1, edge):
                copies.append(remote(place, place, xs.at[slot, 0, i - 1], xr.at[slot, 0, i - 1], a_device(i)))
        elif phase == 1:
            place = gat.at[source, core, beta]
            for i in range(1, edge):
                copies.append(remote(place, place, xs.at[slot, 1, i - 1], xr.at[slot, 1, i - 1], b_device(i)))
        else:
            place = gat.at[source, core]
            copies.append(remote(place, place, xs.at[slot, 2, 0], xr.at[mirror[slot], 2, 0], partner))
        return copies

    spread = {}

    def slot_of(index, h):
        return 0 if h == 0 else 2 * h - 1 + index

    mirror = {slot_of(i, h): slot_of(i if h == half else 1 - i, h) for h in range(1, half + 1) for i in range(2)}
    mirror[0] = 0

    def spread_step(slot, source, phase):
        if phase > 0:
            for copy in spread[mirror[slot] if phase == 3 else slot, phase - 1]:
                copy.wait_recv()
        if phase < 3:
            copies = spread_copies(source, slot, phase)
            for copy in copies:
                copy.start()
            spread[slot, phase] = copies

    out_copies = []
    scale = bs_ref.shape[1] ** (-0.5)

    def coarse_matmul(source):
        lhs = gat[source].reshape(2 * edge * edge * 8, bs_ref.shape[1])
        scores = lax.dot_general(lhs, rep[...], (((1,), (1,)), ((), ())), preferred_element_type=F32) * scale
        scores = scores.reshape(2, edge, edge, 8, scores.shape[-1])
        for b in range(edge):
            for a in range(edge):
                stage[source, b, a, 0] = scores[0, b, a].astype(BF)
                stage[source, a, b, 1] = scores[1, b, a].astype(BF)
        copy = pltpu.make_async_copy(stage.at[source], out_ref.at[source], os_.at[len(out_copies)])
        copy.start()
        out_copies.append(copy)

    def raw_rows(ring_, h):
        if h == 0:
            return bp_ref[...]
        return ring[ring_.index, pl.ds((h - 1) * CHUNKS, CHUNKS)].reshape(bins, width)

    def one_hot(targets, v):
        hit = (targets == v[0:1]) | (targets == v[1:2])
        return jnp.where(hit, 1.0, 0.0).astype(BF)

    def pick(targets, v, values):
        return jnp.dot(one_hot(targets, v), values, preferred_element_type=F32).astype(BF)

    order = [(1, 0)] + [(sign, h) for h in range(1, half) for sign in (1, -1)] + [(1, half)]

    def ring_of(sign):
        return core if sign == 1 else 1 - core

    def extract(ring_, h):
        k = 0 if ring_ is None else slot_of(ring_.index, h)
        targets = lax.broadcasted_iota(I32, (block, bins), 0) + block * grp
        v = v_ref[...] if ring_ is None else vbuf[ring_.index, h - 1]
        ext[k] = pick(targets, v, raw_rows(ring_, h))

    def compact(ring_):
        pieces = []
        for d in range(half, raw_hops, -1):
            first, count = ring_.tail_rows(d)
            dest = group_at(ring_.sign, d - raw_hops)
            pieces.append(lax.broadcasted_iota(I32, (count, bins), 0) + (block * dest + first))
        targets = jnp.concatenate(pieces, axis=0)
        picked = pick(targets, vbuf[ring_.index, raw_hops - 1], raw_rows(ring_, raw_hops))
        at = 0
        for d in range(half, raw_hops, -1):
            _, count = ring_.tail_rows(d)
            dbuf[ring_.index, half - d, pl.ds(0, count)] = picked[at:at + count]
            at += count

    def routed_rows(k, s):
        sign, h = order[k]
        if h <= raw_hops:
            at = 0 if h == 0 else 2 * h - 1 + ring_of(sign)
            return ext[at, pl.ds(s * MOST, MOST)]
        if h < half:
            return cbuf[ring_of(sign), messages.index((h, h)), pl.ds(s * MOST, MOST)]
        for each in rings:
            first, count = each.tail_rows(half)
            if first <= s * MOST < first + count:
                return cbuf[each.index, messages.index((half, half)), pl.ds(s * MOST - first, MOST)]

    per_batch = n // 2
    lanes = per_batch * MOST
    share = mp.shape[1] // m_all

    def fine_matmul(batch):
        for s in range(slots):
            rhs = jnp.concatenate([routed_rows(batch * per_batch + k, s) for k in range(per_batch)], axis=0)
            product = lax.dot_general(mp[s], rhs, (((1,), (1,)), ((), ())), preferred_element_type=F32)
            part[batch, :, s] = product.reshape(m_all, share, lanes)

    def reduce_copy(batch, i):
        to = lax.rem(mem + i, m_all)
        return remote(part.at[batch, to], red.at[batch, i - 1], rs.at[batch], rr.at[batch],
                      {"grp": grp, "mem": to})

    def reduce_start(batch):
        @pl.loop(1, m_all)
        def _(i):
            reduce_copy(batch, i).start()

    def all_reduced(batch, sem):
        whole = red.at[batch]
        return pltpu.make_async_copy(whole, whole, sem)

    returns = {}

    def reduce_finish(batch):
        all_reduced(batch, rr.at[batch]).wait()
        total = part[batch, mem] + jnp.sum(red[batch], axis=0)
        lane = lax.broadcasted_iota(I32, (share, lanes), 1)
        for k in range(per_batch):
            tile = jnp.zeros((share, lanes), F32)
            for s in range(slots):
                moved = pltpu.roll(total[s], (MOST * (s - k)) % lanes, 1)
                tile = jnp.where((lane >= MOST * s) & (lane < MOST * (s + 1)), moved, tile)
            at = batch * per_batch + k
            if at == 0:
                ret[at] = tile
            else:
                sums[at] = tile
        for k in range(per_batch):
            at = batch * per_batch + k
            sign, h = order[at]
            if at > 0:
                copy = remote(sums.at[at], ret.at[at], ts.at[at], tr.at[at],
                              {"grp": lax.rem(grp - sign * h + n, n), "mem": mem})
                copy.start()
                returns[at] = copy

    total_rounds = raw_hops * CHUNKS
    steps = {}

    def at_round(r, action):
        steps.setdefault(r, []).append(action)

    stride = max(1, total_rounds // half)
    for h in range(0, half + 1):
        for ring_ in rings:
            if h > ring_.coarse_hops() or (h == 0 and ring_.index == 1):
                continue
            k = slot_of(ring_.index, h)
            base = stride * h

            def arrive(ring_=ring_, h=h, k=k):
                if h > 0:
                    ring_.coarse[h].wait_recv()
                    if h < ring_.coarse_hops():
                        ring_.send_coarse(h + 1)
                else:
                    own_copy.wait()
                spread_step(k, source_of(ring_, h), 0)

            at_round(base, arrive)
            for phase in (1, 2, 3):
                at_round(base + stride * phase + phase,
                         functools.partial(spread_step, k, source_of(ring_, h), phase))

            def multiply(ring_=ring_, h=h):
                if h == 0:
                    rep_copy.wait()
                coarse_matmul(source_of(ring_, h))

            at_round(base + stride * 3 + 3, multiply)

    at_round(2, functools.partial(extract, None, 0))
    for h in range(1, raw_hops):
        for ring_ in rings:
            at_round((h + 1) * CHUNKS + ring_.index + 1, functools.partial(extract, ring_, h))

    for ring_ in rings:
        ring_.send_coarse(1)
        ring_.send_idx(1)
    for r in range(total_rounds):
        for ring_ in rings:
            if r >= CHUNKS:
                if r % CHUNKS == 0:
                    ring_.idx[r // CHUNKS].wait_recv()
                    ring_.send_idx(r // CHUNKS + 1)
                ring_.raw[r - CHUNKS].wait_recv()
            ring_.send_raw(r)
        for action in steps.pop(r, []):
            action()

    for ring_ in rings:
        ring_.idx[raw_hops].wait_recv()
        for r in range(total_rounds - CHUNKS, total_rounds):
            ring_.raw[r].wait_recv()
        compact(ring_)
        ring_.send_compact(0)

    first_batch = (half - raw_hops) + 1
    at_round(total_rounds + 1, functools.partial(extract, rings[0], raw_hops))
    at_round(total_rounds + 2, functools.partial(extract, rings[1], raw_hops))

    early = set()

    def begin_first():
        mp_copy.wait()
        for h in sorted({h for _, h in order[:per_batch] if h > raw_hops}):
            for ring_ in rings:
                ring_.compact[messages.index((h, h))].wait_recv()
                early.add(h)
        fine_matmul(0)
        reduce_start(0)

    at_round(total_rounds + first_batch + 1, begin_first)
    at_round(total_rounds + first_batch + 5, functools.partial(reduce_finish, 0))

    for k in range(0, len(messages)):
        for ring_ in rings:
            if k > 0:
                ring_.send_compact(k)
        for action in steps.pop(total_rounds + k, []):
            action()
    for r in sorted(steps):
        for action in steps[r]:
            action()

    for h in range(raw_hops + 1, half + 1):
        if h not in early:
            for ring_ in rings:
                ring_.compact[messages.index((h, h))].wait_recv()
    fine_matmul(1)
    reduce_start(1)
    for ring_ in rings:
        ring_.drain()
    for copies in spread.values():
        for copy in copies:
            copy.wait_send()
    for copy in out_copies:
        copy.wait()
    reduce_finish(1)
    for at in returns:
        returns[at].wait_recv()

    gathered = jnp.concatenate([ret[k] for k in range(n)], axis=1)
    high = gathered.astype(BF).astype(F32)
    rest = gathered - high
    middle = rest.astype(BF).astype(F32)
    low = rest - middle
    spare = jnp.zeros((-3 * share % 16, n * lanes), F32)
    lhs = jnp.concatenate([high, middle, low, spare], axis=0).astype(BF)
    q = lax.broadcasted_iota(I32, (lanes, bins), 0)
    targets = []
    for sign, h in order:
        owner = lax.rem(grp + sign * h + n, n)
        targets.append(jnp.where(q < block, q + block * owner, -1))
    targets = jnp.concatenate(targets, axis=0)
    for r in range(2):
        chosen = jnp.where(targets == v_ref[r:r + 1, :], 1.0, 0.0).astype(BF)
        got = jnp.dot(lhs, chosen, preferred_element_type=F32)
        fine_ref[r] = got[0:share] + got[share:2 * share] + got[2 * share:3 * share]

    for batch in range(2):
        all_reduced(batch, rs.at[batch]).wait()
    for at in returns:
        returns[at].wait_send()


def local(bin_sketch, rep_sketch, bin_profile, member_profile, bin_routes, owner_slot, cluster_sizes, raw=RAW):
    bins, width = bin_profile.shape
    slots, members, _ = member_profile.shape
    bin_dev, w = bin_sketch.shape
    reps = rep_sketch.shape[0]
    n, m_all = lax.axis_size("grp"), lax.axis_size("mem")
    edge = int(round((m_all // 2) ** 0.5))
    half = n // 2
    share = members // m_all
    cluster_total = owner_slot.shape[0]
    block = slots * MOST
    lanes = half * MOST
    messages = compact_list(half, raw)

    routes = bin_routes.T.reshape(-1)
    ids = jnp.arange(cluster_total, dtype=I32)
    hit = (routes[:, None] == ids[None, :]).astype(I32)
    storage = jnp.sum(hit * owner_slot[None, :], axis=1)
    size = jnp.sum(hit * cluster_sizes[None, :], axis=1)
    rank = jnp.sum((jnp.cumsum(hit, axis=0) - hit) * hit, axis=1)
    index = (storage * MOST + rank).reshape(2, bins)
    v = jnp.concatenate([index, jnp.full((6, bins), -1, I32)], axis=0)

    z_sends = half + raw + raw * CHUNKS + len(messages)
    cfg = {"n": n, "m": m_all, "edge": edge, "raw": raw}
    vmem = pl.BlockSpec(memory_space=pltpu.VMEM)
    hbm = pl.BlockSpec(memory_space=pl.ANY)
    dma = pltpu.SemaphoreType.DMA
    coarse, fine = pl.pallas_call(
        functools.partial(screen, cfg),
        out_shape=(
            jax.ShapeDtypeStruct((n, edge, edge, 2, bin_dev, reps), BF),
            jax.ShapeDtypeStruct((2, share, bins), F32),
        ),
        in_specs=[vmem, hbm, vmem, hbm, vmem],
        out_specs=(hbm, vmem),
        scratch_shapes=[
            pltpu.VMEM((2, raw * CHUNKS, bins // CHUNKS, width), BF),
            pltpu.VMEM((2, raw, 8, bins), I32),
            pltpu.VMEM((2, len(messages), block, width), BF),
            pltpu.VMEM((2, half - raw, block, width), BF),
            pltpu.VMEM((2 * raw + 1, block, width), BF),
            pltpu.VMEM((n, 2, edge, edge, bin_dev, w), BF),
            pltpu.VMEM((reps, w), BF),
            pltpu.VMEM((slots, members, width), BF),
            pltpu.VMEM((n, edge, edge, 2, bin_dev, reps), BF),
            pltpu.VMEM((2, m_all, slots, share, lanes), F32),
            pltpu.VMEM((2, m_all - 1, slots, share, lanes), F32),
            pltpu.VMEM((n, share, lanes), F32),
            pltpu.VMEM((n, share, lanes), F32),
            dma((2, z_sends)), dma((2, z_sends)),
            dma((n, 3, edge - 1)), dma((n, 3, edge - 1)),
            dma((2,)), dma((2,)),
            dma((n,)), dma((n,)),
            dma((3,)), dma((n,)),
        ],
        compiler_params=pltpu.CompilerParams(
            collective_id=0, has_side_effects=True, vmem_limit_bytes=56 * 1024 * 1024),
    )(bin_sketch, rep_sketch, bin_profile, member_profile, v)
    coarse = coarse.reshape(n * m_all * bin_dev, reps)
    column = lax.axis_index("mem") * share + jnp.arange(share, dtype=I32)
    live = column[None, :, None] < size.reshape(2, 1, bins)
    scaled = jnp.where(live, fine * (width * m_all) ** (-0.5), 0.0)
    return (coarse, scaled.transpose(2, 0, 1))


def solution(mesh):
    return jax.shard_map(
        local,
        mesh=mesh,
        in_specs=(
            P(("grp", "mem"), None),
            P(("grp", "mem"), None),
            P("grp", "mem"),
            P("grp", None, "mem"),
            P("grp", None),
            P(),
            P(),
        ),
        out_specs=(P(None, ("grp", "mem")), P("grp", None, "mem")),
        check_vma=False,
    )
```

time: 225 us -> 112 us (0.50)
  blocking collectives: 122 us -> 0 us
  Pallas kernels: 0 us -> 102 us
  local copies, waits for them, and re-layouts: 31.4 us -> 5.3 us
  waiting for transfers between devices: 25.7 us -> 0 us
  starting transfers between devices: 14.7 us -> 0 us
  between operations: 14.3 us -> 0.66 us
  matrix products: 7.71 us -> 0 us
  other arithmetic: 8.71 us -> 3.43 us
    all_to_all x2 -> x0, blocking collectives: 122 us -> none  [the longest x1 100 us: local(): lax.all_to_all(outgoing, 'grp', split_axis=0, concat_axis=0, tiled=True)]
    pallas_call x0 -> x1, Pallas kernels: none -> 102 us  [local(): pl.pallas_call(functools.partial(screen, cfg), out_shape=(jax.ShapeDtypeS...]
    all_to_all x2 -> x0, waiting for transfers between devices: 25.6 us -> none  [the longest x1 14.1 us: summed_on_arrival(): lax.all_to_all(cut_along(array, dim, length), axis, 0, 0, tiled=True)]
    all_to_all x2 -> x0, starting transfers between devices: 14.7 us -> none  [the longest x1 9.34 us: local(): lax.all_to_all(summed, 'grp', split_axis=0, concat_axis=0, tiled=True)]
    unnamed x16 -> x2, local copies, waits for them, and re-layouts: 16.6 us -> 3.74 us
    dot_general x2 -> x0, matrix products: 7.71 us -> none  [the longest x1 7.1 us: local(): lax.dot_general(lax.all_gather(group_rows, 'grp', axis=0, tiled=True), re...]
    scatter x1 -> x0, local copies, waits for them, and re-layouts: 7.43 us -> none  [local(): jnp.zeros((capacity, width_here), jnp.bfloat16).at[slot_index].set(source)]
    transpose x1 -> x0, local copies, waits for them, and re-layouts: 3.99 us -> none  [local(): jnp.einsum('gsmc,sjc->gsmj', incoming, member_profile, preferred_element_...]
  transfers between devices with their start and end apart: 3 -> 0, of which waited for: 2 -> 0; matrix products, arithmetic and copies ran while one was open for 18% -> 0% of each run, Pallas kernels for 0% -> 0%
where the time goes in v1:
time: 112 us
  Pallas kernels  102 us (91%)
  local copies, waits for them, and re-layouts  5.3 us (5%)
  other arithmetic  3.43 us (3%)
    pallas_call x1, Pallas kernels, local(): pl.pallas_call(functools.partial(screen, cfg), out_shape=(jax.ShapeDtypeS...  102 us
    unnamed x2, local copies, waits for them, and re-layouts  3.74 us

profile of v1, /device:TPU:1, one launch (start us, length us, event | category | flops | bytes accessed | tf_op | source)
XLA Modules:
  0.0 111.8 jit_solution(13566830532352098409)
XLA Ops:
  0.6 0.7 eq.29
  1.3 1.2 %reduce-window.6 = s32[48,4,128]{2,0,1:T(8,128)S(1)} reduce-window(s32[48,4,128]{2,0,1:T(8,128)S(1)} %fusion.3, s32[]{:T(128)} %constant.7.clone.1), window={size=1x1x128 pad=0_0x0_0x127_0}, to_apply=%region_1.0 | reduce-window | flops 3121152 | bytes 196612 | tf_op jit(solution)/shard_map/reduce-window
  2.5 0.2 slice_reduce_fusion
  2.8 0.7 copy.11
  3.5 0.8 select_reduce_fusion
  4.3 0.6 concatenate.3.v_ref
  4.9 102.4 %shard_map.86 = (bf16[16,4,4,2,8,256]{5,4,3,2,1,0:T(8,128)(2,1)}, f32[2,8,256]{2,1,0:T(8,128)}) custom-call(bf16[8,1024]{1,0:T(8,128)(2,1)} %bs_ref.1, bf16[256,1024]{1,0:T(8,128)(2,1)} %rep_hbm.1, bf16[256,1024]{1,0:T(8,128)(2,1)} %bp_ref.1, bf16[3,256,1024]{2,1,0:T(8,128)(2,1)} %mp_hbm.1, s32[8,256]{1,0:T(8,128)} %concatenate.3.v_ref), custom_call_target="tpu_custom_call" | custom-call | tf_op jit(solution)/shard_map/pallas_call | solution.py:448
  107.4 1.4 %select_bitcast_fusion = f32[256,2,8]{0,2,1:T(8,128)} fusion(f32[2,8,256]{2,1,0:T(8,128)} %get-tuple-element.5, s32[2,256]{1,0:T(2,128)S(1)} %lt.16, s32[8]{0:T(128)S(1)} %iota_add_fusion), kind=kLoop, calls=%fused_computation.11 | loop fusion | flops 12288 | bytes 34848 | tf_op jit(solution)/shard_map/transpose | solution.py:483
  108.8 3.0 %copy.14 = bf16[4096,256]{1,0:T(8,128)(2,1)} copy(bf16[4096,256]{1,0:T(8,128)(2,1)} %bitcast.25) | data formatting | bytes 4194304
  (7 shorter events, 0.1 us)

commit v2 on v1

--- a/solution.py
+++ b/solution.py
@@ -11,19 +11,29 @@
 RAW = 3
 CHUNKS = 8
 QUEUE = 3
+LAG = 2
 BF = jnp.bfloat16
 F32 = jnp.float32
 I32 = jnp.int32
 
 
 def compact_list(half, raw):
-    return [(h, d) for h in range(raw + 1, half + 1) for d in range(half, h - 1, -1)]
-
-
-def screen(cfg, bs_ref, rep_hbm, bp_ref, mp_hbm, v_ref, out_ref, fine_ref, *scratch):
+    left = [(h, d) for h in range(raw + 1, half + 1) for d in range(half, h - 1, -1)]
+    order = []
+    while left:
+        ready = [p for p in left if p[0] == raw + 1 or (p[0] - 1, p[1]) in order[: max(0, len(order) - LAG)]]
+        if not ready:
+            ready = [p for p in left if p[0] == raw + 1 or (p[0] - 1, p[1]) in order]
+        best = max(ready, key=lambda p: (p[1], -p[0]))
+        order.append(best)
+        left.remove(best)
+    return order
+
+
+def screen(cfg, bs_ref, rep_hbm, bp_hbm, mp_hbm, routes_ref, owner_ref, size_ref, out_ref, fine_ref, *scratch):
     n, m_all, edge, raw_hops = cfg["n"], cfg["m"], cfg["edge"], cfg["raw"]
-    (ring, vbuf, cbuf, dbuf, ext, gat, rep, mp, stage, part, red, sums, ret,
-     zs, zr, xs, xr, rs, rr, ts, tr, ls, os_) = scratch
+    (bp_ref, v_ref, ring, vbuf, cbuf, dbuf, ext, gat, rep, mp, part, red, sums, ret,
+     zs, zr, xs, xr, rs, rr, ts, tr, ls) = scratch
     half = n // 2
     messages = compact_list(half, raw_hops)
     grp = lax.axis_index("grp")
@@ -66,10 +76,12 @@
         pl.semaphore_signal(barrier, inc=1, device_id=device, device_id_type=pl.DeviceIdType.MESH)
     rep_copy = pltpu.make_async_copy(rep_hbm, rep, ls.at[0])
     mp_copy = pltpu.make_async_copy(mp_hbm, mp, ls.at[1])
+    own_copy = pltpu.make_async_copy(bs_ref, gat.at[grp, core, beta, alpha], ls.at[2])
+    own_copy.start()
+    bp_copy = pltpu.make_async_copy(bp_hbm, bp_ref, ls.at[3])
+    bp_copy.start()
     rep_copy.start()
     mp_copy.start()
-    own_copy = pltpu.make_async_copy(bs_ref, gat.at[grp, core, beta, alpha], ls.at[2])
-    own_copy.start()
     pl.semaphore_wait(barrier, len(greeted))
 
     def remote(src, dst, send_sem, recv_sem, device):
@@ -114,7 +126,7 @@
 
         def send_raw(self, r):
             if r < CHUNKS:
-                src = bp_ref.at[pl.ds(r * rows, rows), :]
+                src = bp_hbm.at[pl.ds(r * rows, rows), :]
             else:
                 src = ring.at[self.index, r - CHUNKS]
             self.raw[r] = self.send(src, ring.at[self.index, r])
@@ -137,6 +149,22 @@
             self.compact[k] = self.send(src, cbuf.at[self.index, k, pl.ds(0, count)])
 
     rings = [Ring(0, 1), Ring(1, -1)]
+
+    def route():
+        clusters = owner_ref.shape[1]
+        routes = jnp.concatenate([routes_ref[0:1], routes_ref[1:2]], axis=1)
+        hit = jnp.where(lax.broadcasted_iota(I32, (clusters, 2 * bins), 0) == routes, 1.0, 0.0)
+        before = (lax.broadcasted_iota(I32, (2 * bins, 2 * bins), 0)
+                  < lax.broadcasted_iota(I32, (2 * bins, 2 * bins), 1))
+        earlier = jnp.dot(hit.astype(BF), jnp.where(before, 1.0, 0.0).astype(BF), preferred_element_type=F32)
+        rank = jnp.sum(hit * earlier, axis=0, keepdims=True)
+        table = jnp.concatenate([owner_ref[...].astype(F32), size_ref[...].astype(F32),
+                                 jnp.zeros((14, clusters), F32)], axis=0)
+        looked = jnp.dot(table.astype(BF), hit.astype(BF), preferred_element_type=F32)
+        index = (looked[0:1] * MOST + rank).astype(I32)
+        v_ref[...] = jnp.concatenate(
+            [index[:, :bins], index[:, bins:], jnp.full((6, bins), -1, I32)], axis=0)
+        return looked[1:2]
 
     def source_of(ring_, h):
         return group_at(-ring_.sign, h)
@@ -174,7 +202,6 @@
                 copy.start()
             spread[slot, phase] = copies
 
-    out_copies = []
     scale = bs_ref.shape[1] ** (-0.5)
 
     def coarse_matmul(source):
@@ -183,11 +210,8 @@
         scores = scores.reshape(2, edge, edge, 8, scores.shape[-1])
         for b in range(edge):
             for a in range(edge):
-                stage[source, b, a, 0] = scores[0, b, a].astype(BF)
-                stage[source, a, b, 1] = scores[1, b, a].astype(BF)
-        copy = pltpu.make_async_copy(stage.at[source], out_ref.at[source], os_.at[len(out_copies)])
-        copy.start()
-        out_copies.append(copy)
+                out_ref[source, b, a, 0] = scores[0, b, a].astype(BF)
+                out_ref[source, a, b, 1] = scores[1, b, a].astype(BF)
 
     def raw_rows(ring_, h):
         if h == 0:
@@ -201,7 +225,12 @@
     def pick(targets, v, values):
         return jnp.dot(one_hot(targets, v), values, preferred_element_type=F32).astype(BF)
 
-    order = [(1, 0)] + [(sign, h) for h in range(1, half) for sign in (1, -1)] + [(1, half)]
+    split = (half + raw_hops) // 2
+    every = [(1, 0)] + [(sign, h) for h in range(1, half) for sign in (1, -1)] + [(1, half)]
+    batches = [[e for e in every if e[1] <= raw_hops], [e for e in every if e[1] > split],
+               [e for e in every if raw_hops < e[1] <= split]]
+    order = sum(batches, [])
+    base_of = [0, len(batches[0]), len(batches[0]) + len(batches[1])]
 
     def ring_of(sign):
         return core if sign == 1 else 1 - core
@@ -212,22 +241,22 @@
         v = v_ref[...] if ring_ is None else vbuf[ring_.index, h - 1]
         ext[k] = pick(targets, v, raw_rows(ring_, h))
 
-    def compact(ring_):
+    def compact(ring_, distances):
         pieces = []
-        for d in range(half, raw_hops, -1):
+        for d in distances:
             first, count = ring_.tail_rows(d)
             dest = group_at(ring_.sign, d - raw_hops)
             pieces.append(lax.broadcasted_iota(I32, (count, bins), 0) + (block * dest + first))
         targets = jnp.concatenate(pieces, axis=0)
         picked = pick(targets, vbuf[ring_.index, raw_hops - 1], raw_rows(ring_, raw_hops))
         at = 0
-        for d in range(half, raw_hops, -1):
+        for d in distances:
             _, count = ring_.tail_rows(d)
             dbuf[ring_.index, half - d, pl.ds(0, count)] = picked[at:at + count]
             at += count
 
     def routed_rows(k, s):
-        sign, h = order[k]
+        sign, h = k
         if h <= raw_hops:
             at = 0 if h == 0 else 2 * h - 1 + ring_of(sign)
             return ext[at, pl.ds(s * MOST, MOST)]
@@ -238,20 +267,34 @@
             if first <= s * MOST < first + count:
                 return cbuf[each.index, messages.index((half, half)), pl.ds(s * MOST - first, MOST)]
 
-    per_batch = n // 2
-    lanes = per_batch * MOST
+    per_tile = half
+    lanes = per_tile * MOST
     share = mp.shape[1] // m_all
 
+    def pieces_of(batch):
+        return [(e, s) for s in range(slots) for e in batches[batch]]
+
+    def tiles_of(batch):
+        return -(-len(pieces_of(batch)) // per_tile)
+
     def fine_matmul(batch):
-        for s in range(slots):
-            rhs = jnp.concatenate([routed_rows(batch * per_batch + k, s) for k in range(per_batch)], axis=0)
-            product = lax.dot_general(mp[s], rhs, (((1,), (1,)), ((), ())), preferred_element_type=F32)
-            part[batch, :, s] = product.reshape(m_all, share, lanes)
+        pieces = pieces_of(batch)
+        for t in range(tiles_of(batch)):
+            here = pieces[t * per_tile:(t + 1) * per_tile]
+            total = None
+            for s in sorted({piece[1] for piece in here}):
+                parts = [routed_rows(e, s) if slot == s else jnp.zeros((MOST, width), BF) for e, slot in here]
+                parts += [jnp.zeros((MOST, width), BF)] * (per_tile - len(here))
+                product = lax.dot_general(mp[s], jnp.concatenate(parts, axis=0), (((1,), (1,)), ((), ())),
+                                          preferred_element_type=F32)
+                total = product if total is None else total + product
+            part[batch, :, t] = total.reshape(m_all, share, lanes)
 
     def reduce_copy(batch, i):
         to = lax.rem(mem + i, m_all)
-        return remote(part.at[batch, to], red.at[batch, i - 1], rs.at[batch], rr.at[batch],
-                      {"grp": grp, "mem": to})
+        count = tiles_of(batch)
+        return remote(part.at[batch, to, pl.ds(0, count)], red.at[batch, i - 1, pl.ds(0, count)],
+                      rs.at[batch], rr.at[batch], {"grp": grp, "mem": to})
 
     def reduce_start(batch):
         @pl.loop(1, m_all)
@@ -259,28 +302,30 @@
             reduce_copy(batch, i).start()
 
     def all_reduced(batch, sem):
-        whole = red.at[batch]
+        whole = red.at[batch, :, pl.ds(0, tiles_of(batch))]
         return pltpu.make_async_copy(whole, whole, sem)
 
     returns = {}
 
     def reduce_finish(batch):
         all_reduced(batch, rr.at[batch]).wait()
-        total = part[batch, mem] + jnp.sum(red[batch], axis=0)
+        count = tiles_of(batch)
+        total = part[batch, mem, pl.ds(0, count)] + jnp.sum(red[batch, :, pl.ds(0, count)], axis=0)
         lane = lax.broadcasted_iota(I32, (share, lanes), 1)
-        for k in range(per_batch):
+        pieces = pieces_of(batch)
+        for k, entry in enumerate(batches[batch]):
             tile = jnp.zeros((share, lanes), F32)
             for s in range(slots):
-                moved = pltpu.roll(total[s], (MOST * (s - k)) % lanes, 1)
+                p = pieces.index((entry, s))
+                moved = pltpu.roll(total[p // per_tile], (MOST * (s - p % per_tile)) % lanes, 1)
                 tile = jnp.where((lane >= MOST * s) & (lane < MOST * (s + 1)), moved, tile)
-            at = batch * per_batch + k
+            at = base_of[batch] + k
             if at == 0:
                 ret[at] = tile
             else:
                 sums[at] = tile
-        for k in range(per_batch):
-            at = batch * per_batch + k
-            sign, h = order[at]
+        for k, (sign, h) in enumerate(batches[batch]):
+            at = base_of[batch] + k
             if at > 0:
                 copy = remote(sums.at[at], ret.at[at], ts.at[at], tr.at[at],
                               {"grp": lax.rem(grp - sign * h + n, n), "mem": mem})
@@ -329,7 +374,16 @@
 
     for ring_ in rings:
         ring_.send_coarse(1)
-        ring_.send_idx(1)
+    sizes = []
+
+    def begin_routes():
+        sizes.append(route())
+        for ring_ in rings:
+            ring_.send_idx(1)
+        bp_copy.wait()
+
+    at_round(1, begin_routes)
+    steps[1] = steps[1][-1:] + steps[1][:-1]
     for r in range(total_rounds):
         for ring_ in rings:
             if r >= CHUNKS:
@@ -345,26 +399,21 @@
         ring_.idx[raw_hops].wait_recv()
         for r in range(total_rounds - CHUNKS, total_rounds):
             ring_.raw[r].wait_recv()
-        compact(ring_)
+        compact(ring_, range(half, split, -1))
         ring_.send_compact(0)
 
-    first_batch = (half - raw_hops) + 1
-    at_round(total_rounds + 1, functools.partial(extract, rings[0], raw_hops))
+    for ring_ in rings:
+        at_round(total_rounds + 1, functools.partial(compact, ring_, range(split, raw_hops, -1)))
+    at_round(total_rounds + 2, functools.partial(extract, rings[0], raw_hops))
     at_round(total_rounds + 2, functools.partial(extract, rings[1], raw_hops))
-
-    early = set()
 
     def begin_first():
         mp_copy.wait()
-        for h in sorted({h for _, h in order[:per_batch] if h > raw_hops}):
-            for ring_ in rings:
-                ring_.compact[messages.index((h, h))].wait_recv()
-                early.add(h)
         fine_matmul(0)
         reduce_start(0)
 
-    at_round(total_rounds + first_batch + 1, begin_first)
-    at_round(total_rounds + first_batch + 5, functools.partial(reduce_finish, 0))
+    at_round(total_rounds + 3, begin_first)
+    at_round(total_rounds + 9, functools.partial(reduce_finish, 0))
 
     for k in range(0, len(messages)):
         for ring_ in rings:
@@ -376,20 +425,19 @@
         for action in steps[r]:
             action()
 
-    for h in range(raw_hops + 1, half + 1):
-        if h not in early:
+    for batch in (1, 2):
+        for h in sorted({h for _, h in batches[batch]}):
             for ring_ in rings:
                 ring_.compact[messages.index((h, h))].wait_recv()
-    fine_matmul(1)
-    reduce_start(1)
+        fine_matmul(batch)
+        reduce_start(batch)
     for ring_ in rings:
         ring_.drain()
     for copies in spread.values():
         for copy in copies:
             copy.wait_send()
-    for copy in out_copies:
-        copy.wait()
     reduce_finish(1)
+    reduce_finish(2)
     for at in returns:
         returns[at].wait_recv()
 
@@ -409,9 +457,12 @@
     for r in range(2):
         chosen = jnp.where(targets == v_ref[r:r + 1, :], 1.0, 0.0).astype(BF)
         got = jnp.dot(lhs, chosen, preferred_element_type=F32)
-        fine_ref[r] = got[0:share] + got[share:2 * share] + got[2 * share:3 * share]
-
-    for batch in range(2):
+        whole = got[0:share] + got[share:2 * share] + got[2 * share:3 * share]
+        column = (lax.broadcasted_iota(I32, (share, bins), 0) + mem * share).astype(F32)
+        live = column < sizes[0][:, r * bins:(r + 1) * bins]
+        fine_ref[r] = jnp.where(live, whole * (width * m_all) ** (-0.5), 0.0)
+
+    for batch in range(3):
         all_reduced(batch, rs.at[batch]).wait()
     for at in returns:
         returns[at].wait_send()
@@ -431,29 +482,22 @@
     lanes = half * MOST
     messages = compact_list(half, raw)
 
-    routes = bin_routes.T.reshape(-1)
-    ids = jnp.arange(cluster_total, dtype=I32)
-    hit = (routes[:, None] == ids[None, :]).astype(I32)
-    storage = jnp.sum(hit * owner_slot[None, :], axis=1)
-    size = jnp.sum(hit * cluster_sizes[None, :], axis=1)
-    rank = jnp.sum((jnp.cumsum(hit, axis=0) - hit) * hit, axis=1)
-    index = (storage * MOST + rank).reshape(2, bins)
-    v = jnp.concatenate([index, jnp.full((6, bins), -1, I32)], axis=0)
-
     z_sends = half + raw + raw * CHUNKS + len(messages)
     cfg = {"n": n, "m": m_all, "edge": edge, "raw": raw}
     vmem = pl.BlockSpec(memory_space=pltpu.VMEM)
-    hbm = pl.BlockSpec(memory_space=pl.ANY)
+    hbm = pl.BlockSpec(memory_space=pltpu.HBM)
     dma = pltpu.SemaphoreType.DMA
     coarse, fine = pl.pallas_call(
         functools.partial(screen, cfg),
         out_shape=(
-            jax.ShapeDtypeStruct((n, edge, edge, 2, bin_dev, reps), BF),
-            jax.ShapeDtypeStruct((2, share, bins), F32),
+            pltpu.VMEM((n, edge, edge, 2, bin_dev, reps), BF),
+            pltpu.VMEM((2, share, bins), F32),
         ),
-        in_specs=[vmem, hbm, vmem, hbm, vmem],
-        out_specs=(hbm, vmem),
+        in_specs=[hbm, hbm, hbm, hbm, vmem, vmem, vmem],
+        out_specs=(vmem, vmem),
         scratch_shapes=[
+            pltpu.VMEM((bins, width), BF),
+            pltpu.VMEM((8, bins), I32),
             pltpu.VMEM((2, raw * CHUNKS, bins // CHUNKS, width), BF),
             pltpu.VMEM((2, raw, 8, bins), I32),
             pltpu.VMEM((2, len(messages), block, width), BF),
@@ -462,25 +506,20 @@
             pltpu.VMEM((n, 2, edge, edge, bin_dev, w), BF),
             pltpu.VMEM((reps, w), BF),
             pltpu.VMEM((slots, members, width), BF),
-            pltpu.VMEM((n, edge, edge, 2, bin_dev, reps), BF),
-            pltpu.VMEM((2, m_all, slots, share, lanes), F32),
-            pltpu.VMEM((2, m_all - 1, slots, share, lanes), F32),
+            pltpu.VMEM((3, m_all, slots, share, lanes), F32),
+            pltpu.VMEM((3, m_all - 1, slots, share, lanes), F32),
             pltpu.VMEM((n, share, lanes), F32),
             pltpu.VMEM((n, share, lanes), F32),
             dma((2, z_sends)), dma((2, z_sends)),
             dma((n, 3, edge - 1)), dma((n, 3, edge - 1)),
-            dma((2,)), dma((2,)),
+            dma((3,)), dma((3,)),
             dma((n,)), dma((n,)),
-            dma((3,)), dma((n,)),
+            dma((4,)),
         ],
         compiler_params=pltpu.CompilerParams(
-            collective_id=0, has_side_effects=True, vmem_limit_bytes=56 * 1024 * 1024),
-    )(bin_sketch, rep_sketch, bin_profile, member_profile, v)
-    coarse = coarse.reshape(n * m_all * bin_dev, reps)
-    column = lax.axis_index("mem") * share + jnp.arange(share, dtype=I32)
-    live = column[None, :, None] < size.reshape(2, 1, bins)
-    scaled = jnp.where(live, fine * (width * m_all) ** (-0.5), 0.0)
-    return (coarse, scaled.transpose(2, 0, 1))
+            collective_id=0, has_side_effects=True, vmem_limit_bytes=64749568),
+    )(bin_sketch, rep_sketch, bin_profile, member_profile, bin_routes.T, owner_slot[None], cluster_sizes[None])
+    return (coarse.reshape(n * m_all * bin_dev, reps), fine.transpose(2, 0, 1))
 
 
 def solution(mesh):

time: 112 us -> 103 us (0.920)
  other arithmetic: 3.43 us -> 0 us
  local copies, waits for them, and re-layouts: 5.3 us -> 1.93 us
    unnamed x2, local copies, waits for them, and re-layouts: 3.74 us -> 1.93 us
    pallas_call x1, Pallas kernels: 102 us -> 101 us  [local(): pl.pallas_call(functools.partial(screen, cfg), out_shape=(pltpu.VMEM((n,...]
    transpose x1 -> x0, other arithmetic: 1.39 us -> none  [local(): return (coarse, scaled.transpose(2, 0, 1))]
    another operation x2 -> x0, other arithmetic: 1.22 us -> none
where the time goes in v2:
time: 103 us
  Pallas kernels  101 us (98%)
  local copies, waits for them, and re-layouts  1.93 us (2%)
    pallas_call x1, Pallas kernels, local(): pl.pallas_call(functools.partial(screen, cfg), out_shape=(pltpu.VMEM((n,...  101 us

profile of v2, /device:TPU:1, one launch (start us, length us, event | category | flops | bytes accessed | tf_op | source)
XLA Modules:
  0.0 103.3 jit_solution(7803013202971212197)
XLA Ops:
  0.6 100.7 %shard_map.86 = (bf16[16,4,4,2,8,256]{5,4,3,2,1,0:T(8,128)(2,1)S(1)}, f32[2,8,256]{2,1,0:T(8,128)S(1)}) custom-call(bf16[8,1024]{1,0:T(8,128)(2,1)} %bs_ref.1, bf16[256,1024]{1,0:T(8,128)(2,1)} %rep_hbm.1, bf16[256,1024]{1,0:T(8,128)(2,1)} %bp_hbm.1, bf16[3,256,1024]{2,1,0:T(8,128)(2,1)} %mp_hbm.1, s32[2,256]{1,0:T(2,128)} %bitcast.7, s32[1,48]{1,0:T(1,128)} %bitcast.8, ...), custom_call_target="tpu_custom_call" | custom-call | tf_op jit(solution)/shard_map/pallas_call | solution.py:490
  101.3 1.3 %copy.11 = bf16[4096,256]{1,0:T(8,128)(2,1)} copy(bf16[4096,256]{1,0:T(8,128)(2,1)S(1)} %bitcast.5) | data formatting | bytes 4194304
  102.7 0.6 copy.12

commit v3 on v2

--- a/solution.py
+++ b/solution.py
@@ -19,6 +19,9 @@
 
 def compact_list(half, raw):
     left = [(h, d) for h in range(raw + 1, half + 1) for d in range(half, h - 1, -1)]
+    if (half, raw) == (8, 3):
+        return [(4, 8), (4, 7), (4, 6), (5, 8), (5, 7), (4, 5), (6, 8), (6, 7), (5, 6), (7, 8), (7, 7), (6, 6),
+                (8, 8), (5, 5), (4, 4)]
     order = []
     while left:
         ready = [p for p in left if p[0] == raw + 1 or (p[0] - 1, p[1]) in order[: max(0, len(order) - LAG)]]
@@ -100,7 +103,7 @@
             if k - self.done >= QUEUE:
                 self.sent[self.done].wait_send()
                 self.done += 1
-            copy = remote(src, dst, zs.at[self.index, k], zr.at[self.index, k], z_device(self.sign))
+            copy = remote(src, dst, zs.at[self.index, k % QUEUE], zr.at[self.index, k], z_device(self.sign))
             copy.start()
             self.sent.append(copy)
             return copy
@@ -174,17 +177,21 @@
         if phase == 0:
             place = gat.at[source, core, beta, alpha]
             for i in range(1, edge):
-                copies.append(remote(place, place, xs.at[slot, 0, i - 1], xr.at[slot, 0, i - 1], a_device(i)))
+                copies.append(remote(place, place, xs.at[0], xr.at[slot, 0], a_device(i)))
         elif phase == 1:
             place = gat.at[source, core, beta]
             for i in range(1, edge):
-                copies.append(remote(place, place, xs.at[slot, 1, i - 1], xr.at[slot, 1, i - 1], b_device(i)))
+                copies.append(remote(place, place, xs.at[1], xr.at[slot, 1], b_device(i)))
         else:
             place = gat.at[source, core]
-            copies.append(remote(place, place, xs.at[slot, 2, 0], xr.at[mirror[slot], 2, 0], partner))
+            copies.append(remote(place, place, xs.at[2], xr.at[mirror[slot], 2], partner))
         return copies
 
-    spread = {}
+    def bytes_of(phase, planes, sem):
+        whole = (gat.at[pl.ds(0, planes), 0, 0, pl.ds(0, edge - 1)],
+                 gat.at[pl.ds(0, planes), 0, pl.ds(0, edge - 1)],
+                 gat.at[pl.ds(0, planes), 0])[phase]
+        return pltpu.make_async_copy(whole, whole, sem)
 
     def slot_of(index, h):
         return 0 if h == 0 else 2 * h - 1 + index
@@ -194,13 +201,10 @@
 
     def spread_step(slot, source, phase):
         if phase > 0:
-            for copy in spread[mirror[slot] if phase == 3 else slot, phase - 1]:
-                copy.wait_recv()
+            bytes_of(phase - 1, 1, xr.at[slot, phase - 1]).wait()
         if phase < 3:
-            copies = spread_copies(source, slot, phase)
-            for copy in copies:
+            for copy in spread_copies(source, slot, phase):
                 copy.start()
-            spread[slot, phase] = copies
 
     scale = bs_ref.shape[1] ** (-0.5)
 
@@ -227,10 +231,10 @@
 
     split = (half + raw_hops) // 2
     every = [(1, 0)] + [(sign, h) for h in range(1, half) for sign in (1, -1)] + [(1, half)]
-    batches = [[e for e in every if e[1] <= raw_hops], [e for e in every if e[1] > split],
-               [e for e in every if raw_hops < e[1] <= split]]
+    batches = [[e for e in every if e[1] <= raw_hops], [e for e in every if e[1] > split]]
+    batches += [[e for e in every if e[1] == h] for h in range(split, raw_hops, -1)]
     order = sum(batches, [])
-    base_of = [0, len(batches[0]), len(batches[0]) + len(batches[1])]
+    base_of = [sum(len(b) for b in batches[:i]) for i in range(len(batches))]
 
     def ring_of(sign):
         return core if sign == 1 else 1 - core
@@ -425,7 +429,7 @@
         for action in steps[r]:
             action()
 
-    for batch in (1, 2):
+    for batch in range(1, len(batches)):
         for h in sorted({h for _, h in batches[batch]}):
             for ring_ in rings:
                 ring_.compact[messages.index((h, h))].wait_recv()
@@ -433,11 +437,10 @@
         reduce_start(batch)
     for ring_ in rings:
         ring_.drain()
-    for copies in spread.values():
-        for copy in copies:
-            copy.wait_send()
-    reduce_finish(1)
-    reduce_finish(2)
+    for phase in range(3):
+        bytes_of(phase, n, xs.at[phase]).wait()
+    for batch in range(1, len(batches)):
+        reduce_finish(batch)
     for at in returns:
         returns[at].wait_recv()
 
@@ -462,7 +465,7 @@
         live = column < sizes[0][:, r * bins:(r + 1) * bins]
         fine_ref[r] = jnp.where(live, whole * (width * m_all) ** (-0.5), 0.0)
 
-    for batch in range(3):
+    for batch in range(len(batches)):
         all_reduced(batch, rs.at[batch]).wait()
     for at in returns:
         returns[at].wait_send()
@@ -482,6 +485,7 @@
     lanes = half * MOST
     messages = compact_list(half, raw)
 
+    groups = 2 + (half + raw) // 2 - raw
     z_sends = half + raw + raw * CHUNKS + len(messages)
     cfg = {"n": n, "m": m_all, "edge": edge, "raw": raw}
     vmem = pl.BlockSpec(memory_space=pltpu.VMEM)
@@ -506,13 +510,13 @@
             pltpu.VMEM((n, 2, edge, edge, bin_dev, w), BF),
             pltpu.VMEM((reps, w), BF),
             pltpu.VMEM((slots, members, width), BF),
-            pltpu.VMEM((3, m_all, slots, share, lanes), F32),
-            pltpu.VMEM((3, m_all - 1, slots, share, lanes), F32),
+            pltpu.VMEM((groups, m_all, slots, share, lanes), F32),
+            pltpu.VMEM((groups, m_all - 1, slots, share, lanes), F32),
             pltpu.VMEM((n, share, lanes), F32),
             pltpu.VMEM((n, share, lanes), F32),
-            dma((2, z_sends)), dma((2, z_sends)),
-            dma((n, 3, edge - 1)), dma((n, 3, edge - 1)),
-            dma((3,)), dma((3,)),
+            dma((2, QUEUE)), dma((2, z_sends)),
+            dma((3,)), dma((n, 3)),
+            dma((groups,)), dma((groups,)),
             dma((n,)), dma((n,)),
             dma((4,)),
         ],

time: 103 us -> 98.4 us (0.955)
  Pallas kernels: 101 us -> 95.7 us
    pallas_call x1, Pallas kernels: 101 us -> 95.7 us  [local(): pl.pallas_call(functools.partial(screen, cfg), out_shape=(pltpu.VMEM((n,...]
where the time goes in v3:
time: 98.4 us; the launch traced here: 98.3 us
  Pallas kernels  95.7 us (97%)
  local copies, waits for them, and re-layouts  1.93 us (2%)
    pallas_call x1, Pallas kernels, local(): pl.pallas_call(functools.partial(screen, cfg), out_shape=(pltpu.VMEM((n,...  95.7 us

profile of v3, /device:TPU:1, one launch (start us, length us, event | category | flops | bytes accessed | tf_op | source)
XLA Modules:
  0.0 98.3 jit_solution(9774255878345436547)
XLA Ops:
  0.6 95.7 %shard_map.86 = (bf16[16,4,4,2,8,256]{5,4,3,2,1,0:T(8,128)(2,1)S(1)}, f32[2,8,256]{2,1,0:T(8,128)S(1)}) custom-call(bf16[8,1024]{1,0:T(8,128)(2,1)} %bs_ref.1, bf16[256,1024]{1,0:T(8,128)(2,1)} %rep_hbm.1, bf16[256,1024]{1,0:T(8,128)(2,1)} %bp_hbm.1, bf16[3,256,1024]{2,1,0:T(8,128)(2,1)} %mp_hbm.1, s32[2,256]{1,0:T(2,128)} %bitcast.7, s32[1,48]{1,0:T(1,128)} %bitcast.8, ...), custom_call_target="tpu_custom_call" | custom-call | tf_op jit(solution)/shard_map/pallas_call | solution.py:494
  96.4 1.3 %copy.11 = bf16[4096,256]{1,0:T(8,128)(2,1)} copy(bf16[4096,256]{1,0:T(8,128)(2,1)S(1)} %bitcast.5) | data formatting | bytes 4194304
  97.7 0.6 copy.12
